TPU v7x, 256 devices: a whole 4x4x8 slice. The times are simulated.
256 devices in a mesh: section: 4 (over x_hi, core), fsdp: 64 (over z, x_lo, y).
Axes of the slice: x: 4 (x_hi: 2, x_lo: 2; x = x_hi * 2 + x_lo), y: 4, z: 8, core: 2. Of those that a mesh axis runs over, the one named last changes fastest.
Arguments:
- signals: bfloat16 [16384, 1536], P('fsdp', 'section'), may hold values from -6 to 6
- conv_weight: bfloat16 [768, 9, 1536], P('fsdp', None, 'section'), may hold values from -0.078125 to 0.078125
- buckets: int32 [2, 2], replicated, may hold values from 0 to 8, as said below
Outputs:
- results: bfloat16 [16384, 1536], P('fsdp', 'section')
- grad_weight: float32 [768, 9, 1536], P('fsdp', None, 'section')
Inputs may be any that keep to these rules, and one draw needn't show every extreme that they name: `buckets`: a bucket b means 16 + 2 b live pixels along that side, in the top left of each sample's grid; microbatch 0 has a height bucket of 5 or more; some entry is 8.
All inputs are finite; a program needn't handle non-finite values.
Results may differ from a plain program's by a relative error of at most 0.0054.
Values may be sent and summed in bfloat16 or wider, within the bound.
No kernel may reach another device: no remote copies, remote signals or barrier semaphores. Data moves between devices by JAX's collectives and lax.ppermute only.
A program may use at most 128 MiB of HBM per device.

v0:
```python
import jax
import jax.numpy as jnp
from jax import lax
from jax.sharding import Mesh
from jax.sharding import PartitionSpec as P

GROUPS = 32
SIDE = 32
MICRO = 2
ROWS_DEV = 8
FSDP = ("fsdp_0", "fsdp_1", "fsdp_2")
eps = 1e-05


def from_partner(value, axis, stride):
    mask = 2**stride
    pairs = [(source, source ^ mask) for source in range(lax.axis_size(axis))]
    return lax.ppermute(value, axis, pairs)


def padded_2(cells, sides, width):
    for axis, dim in sides:
        count = lax.axis_size(axis)
        head = lax.slice_in_dim(cells, 0, width, axis=dim)
        tail = lax.slice_in_dim(cells, cells.shape[dim] - width, cells.shape[dim], axis=dim)
        cells = jnp.concatenate(
            [
                lax.ppermute(tail, axis, [(i, (i + 1) % count) for i in range(count)]),
                cells,
                lax.ppermute(head, axis, [((i + 1) % count, i) for i in range(count)]),
            ],
            axis=dim,
        )
    return cells


def copy_for_each(shard, axis):
    copies = jnp.broadcast_to(shard, (lax.axis_size(axis), *shard.shape))
    return lax.all_to_all(copies, axis, split_axis=0, concat_axis=0, tiled=True)


def over_copies(shard, axis):
    everything = copy_for_each(shard, axis)
    return jnp.sum(everything, axis=0)


def together(arrays, axis):
    ends = [0]
    for a in arrays:
        ends.append(ends[-1] + a.size)
    subtotal = over_copies(jnp.concatenate([a.ravel() for a in arrays]), axis)
    return tuple((subtotal[b:e].reshape(a.shape) for a, b, e in zip(arrays, ends, ends[1:])))


def reduced_to_own(tiles, axes, turns):
    dims = [lax.axis_size(a) for a in axes]
    tiles = tiles.reshape(*dims, *tiles.shape[1:])
    tiles = tiles.transpose(*turns, *range(len(axes), tiles.ndim))
    tiles = tiles.reshape(-1, *tiles.shape[len(axes) :])
    for k in turns:
        tiles = lax.psum_scatter(tiles, axes[k], scatter_dimension=0, tiled=True)
    return tiles[0]


def split_up(shard, dim, length):
    dims = shard.shape
    tiles = shard.reshape(*dims[:dim], length, dims[dim] // length, *dims[dim + 1 :])
    return jnp.moveaxis(tiles, dim, 0)


def sum_by_axis(shard, axes, turns, dim):
    length = lax.axis_size(axes)
    return reduced_to_own(split_up(shard, dim, length), axes, turns)


def silu_slope(value):
    sig = jax.nn.sigmoid(value)
    return sig * (1.0 + value * (1.0 - sig))


def section_swap(value, bit):
    return from_partner(value, "section", bit)


def per_device(signals, conv_weight, buckets):
    tok = signals.shape[0]
    half = signals.shape[1]
    width = 2 * half
    group_width = width // GROUPS
    local_groups = half // group_width
    section_index = lax.axis_index("section")
    upper_half = section_index % 2 == 1
    role_up = section_index >= 2
    fsdp_index = lax.axis_index(FSDP)
    pieces = SIDE // ROWS_DEV
    samples = lax.axis_size(FSDP) // pieces
    shifted = fsdp_index + 1
    sample_id = shifted // pieces % samples
    piece_id = shifted % pieces
    micro_id = sample_id // (samples // MICRO)
    picked_micro = jnp.arange(MICRO) == micro_id
    bucket_h = jnp.sum(jnp.where(picked_micro, buckets[:, 0], 0))
    bucket_w = jnp.sum(jnp.where(picked_micro, buckets[:, 1], 0))
    live_h = 16 + 2 * bucket_h
    live_w = 16 + 2 * bucket_w
    row_ids = piece_id * ROWS_DEV + jnp.arange(ROWS_DEV)
    col_ids = jnp.arange(SIDE)
    mask_grid = ((row_ids[:, None] < live_h) & (col_ids[None, :] < live_w)).astype(jnp.float32)
    mask_flat = mask_grid.reshape(tok, 1)
    group_count = (live_h * live_w).astype(jnp.float32) * group_width
    sample_hot = (jnp.arange(samples) == sample_id).astype(jnp.float32)[:, None]

    def with_rims(field):
        grid = field.reshape(ROWS_DEV, SIDE, field.shape[-1])
        padded = padded_2(grid, ((FSDP, 0),), 1)
        top = jnp.where(piece_id > 0, padded[:1], jnp.zeros_like(padded[:1]))
        bottom = jnp.where(piece_id < pieces - 1, padded[-1:], jnp.zeros_like(padded[-1:]))
        padded = jnp.concatenate([top, padded[1:-1], bottom], axis=0)
        return jnp.pad(padded, ((0, 0), (1, 1), (0, 0)))

    def group_totals(first, second):
        total_first, total_second = together(
            (sample_hot * first[None, :], sample_hot * second[None, :]), FSDP
        )
        return (
            jnp.sum(sample_hot * total_first, axis=0),
            jnp.sum(sample_hot * total_second, axis=0),
        )

    def normalize(values):
        grouped = values.reshape(tok, local_groups, group_width)
        masked = grouped * mask_flat[:, :, None]
        first = jnp.sum(masked, axis=(0, 2))
        second = jnp.sum(masked * masked, axis=(0, 2))
        total_first, total_second = group_totals(first, second)
        mean = total_first / group_count
        spread = total_second / group_count - mean * mean
        scale = lax.rsqrt(spread + eps)
        normed = (grouped - mean[None, :, None]) * scale[None, :, None]
        return (normed.reshape(tok, half), scale)

    def forward(inputs, weights):
        values = inputs.astype(jnp.float32)
        normed, scale = normalize(values)
        activated = (mask_flat * jax.nn.silu(normed)).astype(jnp.bfloat16)
        padded = with_rims(activated)
        partner = section_swap(padded, 0)
        lower = jnp.where(upper_half, partner, padded)
        upper = jnp.where(upper_half, padded, partner)
        full = jnp.concatenate([lower, upper], axis=-1)
        mixed = jnp.zeros((tok, half), jnp.float32)
        for tap in range(9):
            row_off, col_off = (tap // 3, tap % 3)
            slab = full[row_off : row_off + ROWS_DEV, col_off : col_off + SIDE].reshape(tok, width)
            mixed = mixed + jnp.dot(slab, weights[:, tap, :], preferred_element_type=jnp.float32)
        output = (values + mask_flat * mixed).astype(jnp.bfloat16)
        return (output, (normed, scale, full))

    def backward(grads, cache, weights):
        normed, scale, full = cache
        slope = (grads.astype(jnp.float32) * mask_flat).astype(jnp.bfloat16)
        padded = with_rims(slope)
        partial_value = jnp.zeros((tok, width), jnp.float32)
        for tap in range(9):
            row_off, col_off = (tap // 3, tap % 3)
            slab = padded[
                2 - row_off : 2 - row_off + ROWS_DEV, 2 - col_off : 2 - col_off + SIDE
            ].reshape(tok, half)
            partial_value = partial_value + lax.dot_general(
                slab,
                weights[:, tap, :],
                (((1,), (1,)), ((), ())),
                preferred_element_type=jnp.float32,
            )
        keep = jnp.where(upper_half, partial_value[:, half:], partial_value[:, :half])
        send = jnp.where(upper_half, partial_value[:, :half], partial_value[:, half:]).astype(
            jnp.bfloat16
        )
        arrived = section_swap(send, 0)
        kept = lax.optimization_barrier(keep.astype(jnp.bfloat16)).astype(jnp.float32)
        upstream = kept + arrived.astype(jnp.float32)
        gated = mask_flat * upstream * silu_slope(normed)
        grouped = gated.reshape(tok, local_groups, group_width)
        normed_grouped = normed.reshape(tok, local_groups, group_width)
        first = jnp.sum(grouped, axis=(0, 2))
        second = jnp.sum(grouped * normed_grouped, axis=(0, 2))
        total_first, total_second = group_totals(first, second)
        centred = (
            grouped
            - (total_first / group_count)[None, :, None]
            - normed_grouped * (total_second / group_count)[None, :, None]
        )
        through = mask_flat * (scale[None, :, None] * centred).reshape(tok, half)
        return (grads.astype(jnp.float32) + through, slope)

    weights = lax.all_gather(conv_weight, FSDP, axis=0, tiled=True)
    start = (signals.astype(jnp.float32) * mask_flat).astype(jnp.bfloat16)
    first_out, first_cache = forward(start, weights)
    handed = section_swap(first_out, 1)
    second_out, second_cache = forward(handed, weights)
    up_grads, up_slope = backward(signals, second_cache, weights)
    returned = section_swap(up_grads.astype(jnp.bfloat16), 1)
    down_grads, down_slope = backward(returned, first_cache, weights)
    results = jnp.where(role_up, second_out, (mask_flat * down_grads).astype(jnp.bfloat16))
    chosen_full = jnp.where(role_up, second_cache[2], first_cache[2])
    chosen_slope = jnp.where(role_up, up_slope, down_slope)
    taps = []
    for tap in range(9):
        row_off, col_off = (tap // 3, tap % 3)
        slab = chosen_full[row_off : row_off + ROWS_DEV, col_off : col_off + SIDE].reshape(
            tok, width
        )
        taps.append(
            lax.dot_general(
                slab, chosen_slope, (((0,), (0,)), ((), ())), preferred_element_type=jnp.float32
            )
        )
    grad_weight = sum_by_axis(jnp.stack(taps, axis=1), FSDP, (0, 2, 1), 0)
    return (results, grad_weight)


def solution(mesh):
    finer = Mesh(
        mesh.devices.reshape(mesh.shape["section"], 8, 2, 4),
        ("section", "fsdp_0", "fsdp_1", "fsdp_2"),
    )
    placed = (P(FSDP, "section"), P(FSDP, None, "section"), P())
    return jax.shard_map(
        per_device,
        mesh=finer,
        in_specs=placed,
        out_specs=(P(FSDP, "section"), P(FSDP, None, "section")),
        check_vma=False,
    )
```

profile of v0, /device:TPU:1, one launch (start us, length us, event | category | flops | bytes accessed | tf_op | source)
XLA Modules:
  0.0 720.2 jit_solution(4324919274513506607)
XLA Ops:
  13.1 9.8 %collective-permute-start.8 = (bf16[1,32,384]{2,1,0:T(8,128)(2,1)S(1)}, bf16[1,32,384]{2,1,0:T(8,128)(2,1)S(1)}, u32[]{:S(2)}, u32[]{:S(2)}) collective-permute-start(bf16[1,32,384]{2,1,0:T(8,128)(2,1)S(1)} %get-tuple-element.96), channel_id=1, source_target_pairs={{1,0},{2,1},{3,2},{4,3},{5,4},{6,5},{7,6},{8,7},{9,8},{10,9},{11,1... | collective-permute-start | bytes 73736 | tf_op jit(solution)/shard_map/ppermute | solution.py:30
  24.3 4.6 all-to-all-start
  30.0 8.2 %collective-permute-done.7 = bf16[1,32,384]{2,1,0:T(8,128)(2,1)S(1)} collective-permute-done((bf16[1,32,384]{2,1,0:T(8,128)(2,1)S(1)}, bf16[1,32,384]{2,1,0:T(8,128)(2,1)S(1)}, u32[]{:S(2)}, u32[]{:S(2)}) %collective-permute-start.7) | collective-permute-done | bytes 24608 | tf_op jit(solution)/shard_map/ppermute | solution.py:28
  43.2 6.4 collective-permute-done
  49.8 3.6 collective-permute-start.2
  54.8 1.9 fusion.74
  56.7 227.4 %all-gather.2.cloned.1.call-done = bf16[768,9,384]{2,1,0:T(8,128)(2,1)} async-done(((bf16[12,9,384]{2,1,0:T(8,128)(2,1)}), bf16[768,9,384]{2,1,0:T(8,128)(2,1)}) %all-gather.2.cloned.1.call-update) | async-done | bytes 5308432 | tf_op jit(solution)/shard_map/all_gather | solution.py:196
  284.1 20.1 %fusion.92 = (bf16[768,1,384]{2,1,0:T(2,128)(2,1)S(1)}, bf16[768,1,384]{2,1,0:T(2,128)(2,1)S(1)}, bf16[768,1,384]{2,1,0:T(2,128)(2,1)S(1)}, bf16[768,1,384]{2,1,...) fusion(bf16[768,9,384]{2,1,0:T(8,128)(2,1)} %all-gather.2.clone, ...), kind=kLoop, calls=%fused_computation.263 | loop fusion | bytes 10616832 | tf_op jit(solution)/shard_map/slice | solution.py:155
  311.0 3.0 collective-permute-start.3
  328.2 7.3 %all-to-all-start.1 = ((f32[64,1,512]{2,1,0:T(1,128)}), f32[64,1,512]{2,1,0:T(1,128)}, u32[]{:S(2)}, u32[]{:S(2)}) async-start(f32[64,1,512]{2,1,0:T(1,128)} %broadcast_in_dim.15), calls=%async_computation.1 | async-start | bytes 262144 | tf_op jit(solution)/shard_map/all_to_all | solution.py:39
  338.0 43.5 %collective-permute-start.9 = (bf16[256,384]{1,0:T(8,128)(2,1)}, bf16[256,384]{1,0:T(8,128)(2,1)}, u32[]{:S(2)}, u32[]{:S(2)}) collective-permute-start(bf16[256,384]{1,0:T(8,128)(2,1)} %get-tuple-element.74), channel_id=1, source_target_pairs={{0,64},{64,0},{128,192},{192,128},{1,65},{65,1},{129,193},{193,129... | collective-permute-start | bytes 589832 | tf_op jit(solution)/shard_map/ppermute | solution.py:18
  388.7 2.5 fusion.87
  393.4 20.4 %all_to_all.24 = f32[64,1,512]{2,1,0:T(1,128)S(1)} all-to-all(f32[64,1,512]{2,1,0:T(1,128)S(1)} %broadcast_in_dim.16), channel_id=1, replica_groups=mesh['section'=4,'fsdp_0'=8,'fsdp_1'=2,'fsdp_2'=4] {'fsdp_0','fsdp_1','f..., dimensions={0} | all-to-all | bytes 262144 | tf_op jit(solution)/shard_map/all_to_all | solution.py:39
  417.0 1.8 collective-permute-start.5
  418.8 1.8 collective-permute-start.10
  420.6 5.2 collective-permute-done.4
  426.7 4.1 collective-permute-start.6
  435.6 1.9 fusion.93
  437.5 1.9 copy.104
  439.5 1.9 dot_general.226
  441.4 1.9 copy.105
  443.3 1.9 dot_general.230
  445.2 1.9 copy.106
  447.1 1.9 dot_general.234
  449.0 1.9 copy.107
  450.9 1.9 dot_general.238
  452.8 1.9 copy.108
  454.7 1.9 dot_general.242
  456.6 1.9 copy.109
  458.5 1.9 dot_general.246
  460.4 1.9 copy.110
  462.3 1.9 dot_general.250
  464.2 1.9 copy.111
  466.1 1.9 dot_general.254
  468.0 1.9 copy.112
  469.9 1.9 dot_general.258
  481.0 11.2 %copy.113 = f32[8,4,2,12,9,384]{5,2,1,0,4,3:T(2,128)} copy(f32[8,4,2,12,9,384]{5,3,1,2,0,4:T(8,128)S(1)} %bitcast.228) | data formatting | bytes 21233664 | tf_op jit(solution)/shard_map/transpose | solution.py:58
  492.3 13.5 %reshape.540 = f32[64,12,9,384]{3,0,2,1:T(8,128)} reshape(f32[8,4,2,12,9,384]{5,2,1,0,4,3:T(2,128)} %copy.113) | data formatting | bytes 21233664 | tf_op jit(solution)/shard_map/reshape | solution.py:59
  509.6 5.9 collective-permute-done.11
  521.8 4.8 collective-permute-start.13
  530.8 85.7 %reduce-scatter.4.cloned.1.call-done = f32[8,12,9,384]{3,0,2,1:T(8,128)} async-done(((f32[64,12,9,384]{3,0,2,1:T(8,128)}), f32[8,12,9,384]{3,0,2,1:T(8,128)}) %reduce-scatter.4.cloned.1.call-update) | async-done | bytes 1327120 | tf_op jit(solution)/shard_map/reduce_scatter | solution.py:61
  619.2 8.6 %all-to-all-start.3 = ((f32[64,1,512]{2,1,0:T(1,128)}), f32[64,1,512]{2,1,0:T(1,128)S(1)}, u32[]{:S(2)}, u32[]{:S(2)}) async-start(f32[64,1,512]{2,1,0:T(1,128)} %broadcast_in_dim.17), calls=%async_computation.3 | async-start | bytes 262144 | tf_op jit(solution)/shard_map/all_to_all | solution.py:39
  628.2 9.3 %all-to-all-done.3 = f32[64,1,512]{2,1,0:T(1,128)S(1)} async-done(((f32[64,1,512]{2,1,0:T(1,128)}), f32[64,1,512]{2,1,0:T(1,128)S(1)}, u32[]{:S(2)}, u32[]{:S(2)}) %all-to-all-start.3) | async-done | bytes 131104 | tf_op jit(solution)/shard_map/all_to_all | solution.py:39
  637.9 32.5 %all-reduce.9.cloned.1.call-done = f32[8,12,9,384]{3,0,2,1:T(8,128)} async-done(((f32[8,12,9,384]{3,0,2,1:T(8,128)}), f32[8,12,9,384]{3,0,2,1:T(8,128)}) %all-reduce.9.cloned.1.call-update) | async-done | bytes 1327120
  670.5 2.2 constant_dynamic-slice_fusion.1
  673.0 2.2 fusion.7
  675.2 35.8 %all-reduce.11.cloned.1.call-done = f32[2,12,9,384]{3,0,2,1:T(2,128)} async-done(((f32[2,12,9,384]{3,0,2,1:T(2,128)}), f32[2,12,9,384]{3,0,2,1:T(2,128)}) %all-reduce.11.cloned.1.call-update) | async-done | bytes 331792
  711.0 1.7 constant_dynamic-slice_fusion
  (302 shorter events, 81.9 us)
Async XLA Ops:
  7.2 277.0 %all-gather.2.cloned.1.call-start = ((), (), s32[]{:S(2)}) async-start(), calls=%async_computation.5 | async-start | bytes 9584640 | tf_op jit(solution)/shard_map/all_gather | solution.py:196
  13.1 16.9 %collective-permute-start.8 = (bf16[1,32,384]{2,1,0:T(8,128)(2,1)S(1)}, bf16[1,32,384]{2,1,0:T(8,128)(2,1)S(1)}, u32[]{:S(2)}, u32[]{:S(2)}) collective-permute-start(bf16[1,32,384]{2,1,0:T(8,128)(2,1)S(1)} %get-tuple-element.96), channel_id=1, source_target_pairs={{1,0},{2,1},{3,2},{4,3},{5,4},{6,5},{7,6},{8,7},{9,8},{10,9},{11,1... | collective-permute-start | bytes 73736 | tf_op jit(solution)/shard_map/ppermute | solution.py:30
  24.3 14.5 %all-to-all-start = ((f32[64,1,512]{2,1,0:T(1,128)}), f32[64,1,512]{2,1,0:T(1,128)S(1)}, u32[]{:S(2)}, u32[]{:S(2)}) async-start(f32[64,1,512]{2,1,0:T(1,128)} %broadcast_in_dim.14), calls=%async_computation | async-start | bytes 262144 | tf_op jit(solution)/shard_map/all_to_all | solution.py:39
  29.0 9.1 %collective-permute-start.7 = (bf16[1,32,384]{2,1,0:T(8,128)(2,1)S(1)}, bf16[1,32,384]{2,1,0:T(8,128)(2,1)S(1)}, u32[]{:S(2)}, u32[]{:S(2)}) collective-permute-start(bf16[1,32,384]{2,1,0:T(8,128)(2,1)S(1)} %get-tuple-element.95), channel_id=1, source_target_pairs={{0,1},{1,2},{2,3},{3,4},{4,5},{5,6},{6,7},{7,8},{8,9},{9,10},{10,1... | collective-permute-start | bytes 73736 | tf_op jit(solution)/shard_map/ppermute | solution.py:28
  40.1 3.1 collective-permute-start.1
  42.6 7.0 collective-permute-start
  49.8 4.8 collective-permute-start.2
  54.8 2.0 copy-start.9
  54.8 2.0 copy-start.10
  304.5 9.9 %copy-start.4 = (bf16[768,384]{1,0:T(8,128)(2,1)}, bf16[768,384]{1,0:T(8,128)(2,1)S(1)}, u32[]{:S(2)}) copy-start(bf16[768,384]{1,0:T(8,128)(2,1)S(1)} %get-tuple-element.126) | copy-start | bytes 1769476
  304.6 10.3 %copy-start = (bf16[768,384]{1,0:T(8,128)(2,1)}, bf16[768,384]{1,0:T(8,128)(2,1)S(1)}, u32[]{:S(2)}) copy-start(bf16[768,384]{1,0:T(8,128)(2,1)S(1)} %get-tuple-element.125) | copy-start | bytes 1769476
  305.9 9.9 %copy-start.2 = (bf16[768,384]{1,0:T(8,128)(2,1)}, bf16[768,384]{1,0:T(8,128)(2,1)S(1)}, u32[]{:S(2)}) copy-start(bf16[768,384]{1,0:T(8,128)(2,1)S(1)} %get-tuple-element.124) | copy-start | bytes 1769476
  306.3 4.1 copy-start.6
  306.4 1.2 copy-start.30
  310.0 4.0 copy-start.38
  310.6 3.8 copy-start.40
  311.0 8.7 %collective-permute-start.3 = (bf16[256,384]{1,0:T(8,128)(2,1)S(1)}, bf16[256,384]{1,0:T(8,128)(2,1)S(1)}, u32[]{:S(2)}, u32[]{:S(2)}) collective-permute-start(bf16[256,384]{1,0:T(8,128)(2,1)S(1)} %fusion.5), channel_id=1, source_target_pairs={{0,128},{64,192},{128,0},{192,64},{1,129},{65,193},{129,1},{193,65... | collective-permute-start | bytes 589832 | tf_op jit(solution)/shard_map/ppermute | solution.py:18
  318.0 17.6 %copy-start.42 = (bf16[8,32,384]{2,1,0:T(8,128)(2,1)S(1)}, bf16[8,32,384]{2,1,0:T(8,128)(2,1)}, u32[]{:S(2)}) copy-start(bf16[8,32,384]{2,1,0:T(8,128)(2,1)} %get-tuple-element.81) | copy-start | bytes 589828
  319.8 96.0 %copy-start.24 = (bf16[256,384]{1,0:T(8,128)(2,1)}, bf16[256,384]{1,0:T(8,128)(2,1)S(1)}, u32[]{:S(2)}) copy-start(bf16[256,384]{1,0:T(8,128)(2,1)S(1)} %collective-permute-done.3) | copy-start | bytes 589828
  328.2 53.3 %all-to-all-start.1 = ((f32[64,1,512]{2,1,0:T(1,128)}), f32[64,1,512]{2,1,0:T(1,128)}, u32[]{:S(2)}, u32[]{:S(2)}) async-start(f32[64,1,512]{2,1,0:T(1,128)} %broadcast_in_dim.15), calls=%async_computation.1 | async-start | bytes 262144 | tf_op jit(solution)/shard_map/all_to_all | solution.py:39
  335.5 281.0 %reduce-scatter.4.cloned.1.call-start = ((), (), s32[]{:S(2)}) async-start(), calls=%async_computation.6 | async-start | bytes 11943936 | tf_op jit(solution)/shard_map/reduce_scatter | solution.py:61
  338.0 50.8 %collective-permute-start.9 = (bf16[256,384]{1,0:T(8,128)(2,1)}, bf16[256,384]{1,0:T(8,128)(2,1)}, u32[]{:S(2)}, u32[]{:S(2)}) collective-permute-start(bf16[256,384]{1,0:T(8,128)(2,1)} %get-tuple-element.74), channel_id=1, source_target_pairs={{0,64},{64,0},{128,192},{192,128},{1,65},{65,1},{129,193},{193,129... | collective-permute-start | bytes 589832 | tf_op jit(solution)/shard_map/ppermute | solution.py:18
  388.7 27.0 %copy-start.49 = (f32[384]{0:T(512)S(1)}, f32[384]{0:T(512)}, u32[]{:S(2)}) copy-start(f32[384]{0:T(512)} %mul.444) | copy-start | bytes 4612
  388.7 27.0 %copy-start.50 = (f32[384]{0:T(512)S(1)}, f32[384]{0:T(512)}, u32[]{:S(2)}) copy-start(f32[384]{0:T(512)} %sub.99) | copy-start | bytes 4612
  417.0 8.8 %copy-start.23 = (bf16[256,384]{1,0:T(8,128)(2,1)}, bf16[256,384]{1,0:T(8,128)(2,1)S(1)}, u32[]{:S(2)}) copy-start(bf16[256,384]{1,0:T(8,128)(2,1)S(1)} %get-tuple-element.88) | copy-start | bytes 589828
  417.0 3.6 collective-permute-start.5
  418.8 7.0 collective-permute-start.4
  418.8 12.0 %collective-permute-start.10 = (bf16[256,384]{1,0:T(8,128)(2,1)S(1)}, bf16[256,384]{1,0:T(8,128)(2,1)}, u32[]{:S(2)}, u32[]{:S(2)}) collective-permute-start(bf16[256,384]{1,0:T(8,128)(2,1)S(1)} %get-tuple-element.87), channel_id=1, source_target_pairs={{0,128},{64,192},{128,0},{192,64},{1,129},{65,193},{129,1},{193,65... | collective-permute-start | bytes 589832 | tf_op jit(solution)/shard_map/ppermute | solution.py:18
  420.6 6.0 copy-start.43
  426.7 5.7 collective-permute-start.6
  471.8 1.5 copy-start.15
  505.8 1.3 copy-start.51
  505.8 164.7 %all-reduce.9.cloned.1.call-start = ((), (), s32[]{:S(2)}) async-start(), calls=%async_computation.7 | async-start | bytes 2654208
  505.9 3.7 collective-permute-start.12
  508.3 7.2 collective-permute-start.11
  516.6 1.1 copy-start.1
  517.3 1.1 copy-start.3
  519.5 1.1 copy-start.7
  520.0 6.7 copy-start.12
  520.0 6.7 copy-start.14
  521.8 94.7 %collective-permute-start.13 = (bf16[256,384]{1,0:T(8,128)(2,1)}, bf16[256,384]{1,0:T(8,128)(2,1)}, u32[]{:S(2)}, u32[]{:S(2)}) collective-permute-start(bf16[256,384]{1,0:T(8,128)(2,1)} %get-tuple-element.72), channel_id=1, source_target_pairs={{0,64},{64,0},{128,192},{192,128},{1,65},{65,1},{129,193},{193,129... | collective-permute-start | bytes 589832 | tf_op jit(solution)/shard_map/ppermute | solution.py:18
  530.4 86.1 %copy-start.41 = (bf16[256,384]{1,0:T(8,128)(2,1)S(1)}, bf16[256,384]{1,0:T(8,128)(2,1)}, u32[]{:S(2)}) copy-start(bf16[256,384]{1,0:T(8,128)(2,1)} %get-tuple-element.71) | copy-start | bytes 589828
  530.4 86.1 %copy-start.46 = (f32[384]{0:T(512)S(1)}, f32[384]{0:T(512)}, u32[]{:S(2)}) copy-start(f32[384]{0:T(512)} %copy-done.45) | copy-start | bytes 4612
  530.4 86.1 %copy-start.48 = (f32[384]{0:T(512)S(1)}, f32[384]{0:T(512)}, u32[]{:S(2)}) copy-start(f32[384]{0:T(512)} %copy-done.47) | copy-start | bytes 4612
  619.2 53.9 %copy-start.8 = (bf16[768,384]{1,0:T(8,128)(2,1)S(1)}, bf16[768,384]{1,0:T(8,128)(2,1)}, u32[]{:S(2)}) copy-start(bf16[768,384]{1,0:T(8,128)(2,1)} %copy-done.6) | copy-start | bytes 1769476
  619.2 53.9 %copy-start.25 = (bf16[256,384]{1,0:T(8,128)(2,1)S(1)}, bf16[256,384]{1,0:T(8,128)(2,1)}, u32[]{:S(2)}) copy-start(bf16[256,384]{1,0:T(8,128)(2,1)} %copy-done.24) | copy-start | bytes 589828
  619.2 18.4 %all-to-all-start.3 = ((f32[64,1,512]{2,1,0:T(1,128)}), f32[64,1,512]{2,1,0:T(1,128)S(1)}, u32[]{:S(2)}, u32[]{:S(2)}) async-start(f32[64,1,512]{2,1,0:T(1,128)} %broadcast_in_dim.17), calls=%async_computation.3 | async-start | bytes 262144 | tf_op jit(solution)/shard_map/all_to_all | solution.py:39
  627.8 83.2 %all-reduce.11.cloned.1.call-start = ((), (), s32[]{:S(2)}) async-start(), calls=%async_computation.8 | async-start | bytes 663552
  (26 other events, 24.4 us)
Sparse Core Ops, SparseCore 0:
  9.8 274.3 all-gather.1
  505.9 110.5 reduce-scatter.3
  618.9 51.5 all-reduce.8
  672.9 38.0 all-reduce.10
where the time goes:
time: 727 us; the launch traced here: 720 us
  waiting for transfers between devices  418 us (57%)
  local copies, waits for them, and re-layouts  119 us (16%)
  starting transfers between devices  97.2 us (13%)
  other arithmetic  25.8 us (4%)
  matrix products  22.6 us (3%)
  blocking collectives  20.4 us (3%)
  between operations  17 us (2%)
    all_gather x1, waiting for transfers between devices, per_device(): weights = lax.all_gather(conv_weight, FSDP, axis=0, tiled=True)  227 us
    reduce_scatter x1, waiting for transfers between devices, reduced_to_own(): tiles = lax.psum_scatter(tiles, axes[k], scatter_dimension=0, tiled=True)  85.7 us
    unnamed x6, waiting for transfers between devices  68.4 us
    ppermute x6, starting transfers between devices, from_partner(): return lax.ppermute(value, axis, pairs)  60.8 us
    dot_general x18, local copies, waits for them, and re-layouts, per_device(): lax.dot_general(slab, chosen_slope, (((0,), (0,)), ((), ())), preferred_e...  34.2 us
    ppermute x4, waiting for transfers between devices, padded_2(): lax.ppermute(tail, axis, [(i, (i + 1) % count) for i in range(count)])  25.7 us
    all_to_all x3, starting transfers between devices, copy_for_each(): return lax.all_to_all(copies, axis, split_axis=0, concat_axis=0, tiled=True)  20.5 us
    all_to_all x1, blocking collectives, copy_for_each(): return lax.all_to_all(copies, axis, split_axis=0, concat_axis=0, tiled=True)  20.4 us
  transfers between devices with their start and end apart: 21, of which 13 were waited for; matrix products, arithmetic and copies ran while one was open for 6% of the time, Pallas kernels for 0%

commit v1 on v0

--- a/solution.py
+++ b/solution.py
@@ -193,7 +193,9 @@
         through = mask_flat * (scale[None, :, None] * centred).reshape(tok, half)
         return (grads.astype(jnp.float32) + through, slope)
 
-    weights = lax.all_gather(conv_weight, FSDP, axis=0, tiled=True)
+    weights = jnp.concatenate(
+        lax.all_to_all(jnp.stack([conv_weight] * lax.axis_size(FSDP)), FSDP, 0, 0), axis=0
+    )
     start = (signals.astype(jnp.float32) * mask_flat).astype(jnp.bfloat16)
     first_out, first_cache = forward(start, weights)
     handed = section_swap(first_out, 1)

time: 727 us -> 585 us (0.80)
  waiting for transfers between devices: 418 us -> 332 us
  starting transfers between devices: 97.2 us -> 58.6 us
  local copies, waits for them, and re-layouts: 119 us -> 88.7 us
  blocking collectives: 20.4 us -> 37.5 us
  other arithmetic: 25.8 us -> 10.9 us
  matrix products: 22.6 us -> 33.1 us
    all_gather x1 -> x0, waiting for transfers between devices: 227 us -> none  [per_device(): weights = lax.all_gather(conv_weight, FSDP, axis=0, tiled=True)]
    ppermute x4, waiting for transfers between devices: 0.58 us -> 142 us  [padded_2(): lax.ppermute(head, axis, [((i + 1) % count, i) for i in range(count)])]
    ppermute x6, starting transfers between devices: 60.8 us -> 20.9 us  [from_partner(): return lax.ppermute(value, axis, pairs)]
    slice x1 -> x0, local copies, waits for them, and re-layouts: 20.1 us -> none  [forward(): weights[:, tap, :]]
    all_to_all x1 -> x2, blocking collectives: 20.4 us -> 37.5 us  [copy_for_each(): return lax.all_to_all(copies, axis, split_axis=0, concat_axis=0, tiled=True)]
    unnamed x112 -> x48, local copies, waits for them, and re-layouts: 18.5 us -> 6.06 us
    reshape x0 -> x1, local copies, waits for them, and re-layouts: none -> 9.53 us  [per_device(): jnp.concatenate(lax.all_to_all(jnp.stack([conv_weight] * lax.axis_size(FS...]
    all_to_all x3 -> x2, waiting for transfers between devices: 10 us -> 14.8 us  [copy_for_each(): return lax.all_to_all(copies, axis, split_axis=0, concat_axis=0, tiled=True)]
  transfers between devices with their start and end apart: 21 -> 20, of which waited for: 13 -> 14; matrix products, arithmetic and copies ran while one was open for 6% -> 5% of each run, Pallas kernels for 0% -> 0%
where the time goes in v1:
time: 585 us; the launch traced here: 577 us
  waiting for transfers between devices  332 us (57%)
  local copies, waits for them, and re-layouts  88.7 us (15%)
  starting transfers between devices  58.6 us (10%)
  blocking collectives  37.5 us (6%)
  matrix products  33.1 us (6%)
  between operations  16.9 us (3%)
  other arithmetic  10.9 us (2%)
    ppermute x4, waiting for transfers between devices, padded_2(): lax.ppermute(head, axis, [((i + 1) % count, i) for i in range(count)])  142 us
    reduce_scatter x1, waiting for transfers between devices, reduced_to_own(): tiles = lax.psum_scatter(tiles, axes[k], scatter_dimension=0, tiled=True)  84.6 us
    unnamed x5, waiting for transfers between devices  68.6 us
    all_to_all x2, blocking collectives, copy_for_each(): return lax.all_to_all(copies, axis, split_axis=0, concat_axis=0, tiled=True)  37.5 us
    dot_general x18, local copies, waits for them, and re-layouts, per_device(): lax.dot_general(slab, chosen_slope, (((0,), (0,)), ((), ())), preferred_e...  27.8 us
    ppermute x6, starting transfers between devices, from_partner(): return lax.ppermute(value, axis, pairs)  20.9 us
    ppermute x4, waiting for transfers between devices, padded_2(): lax.ppermute(tail, axis, [(i, (i + 1) % count) for i in range(count)])  19.9 us
    all_to_all x2, starting transfers between devices, copy_for_each(): return lax.all_to_all(copies, axis, split_axis=0, concat_axis=0, tiled=True)  18.9 us
  transfers between devices with their start and end apart: 20, of which 14 were waited for; matrix products, arithmetic and copies ran while one was open for 5% of the time, Pallas kernels for 0%

profile of v1, /device:TPU:1, one launch (start us, length us, event | category | flops | bytes accessed | tf_op | source)
XLA Modules:
  0.0 577.5 jit_solution(7129339214259562767)
XLA Ops:
  12.2 23.2 %all_to_all.29 = f32[64,1,512]{2,1,0:T(1,128)S(1)} all-to-all(f32[64,1,512]{2,1,0:T(1,128)S(1)} %broadcast_in_dim.14), channel_id=1, replica_groups=mesh['section'=4,'fsdp_0'=8,'fsdp_1'=2,'fsdp_2'=4] {'fsdp_0','fsdp_1','f..., dimensions={0} | all-to-all | bytes 262144 | tf_op jit(solution)/shard_map/all_to_all | solution.py:39
  35.4 4.4 stack.4
  39.8 5.7 all-to-all-start.1
  45.6 5.6 collective-permute-start.8
  51.1 141.3 %collective-permute-done.8 = bf16[1,32,384]{2,1,0:T(8,128)(2,1)S(1)} collective-permute-done((bf16[1,32,384]{2,1,0:T(8,128)(2,1)S(1)}, bf16[1,32,384]{2,1,0:T(8,128)(2,1)S(1)}, u32[]{:S(2)}, u32[]{:S(2)}) %collective-permute-start.8) | collective-permute-done | bytes 24608 | tf_op jit(solution)/shard_map/ppermute | solution.py:30
  192.5 2.7 collective-permute-done.7
  196.1 4.1 collective-permute-start.1
  201.2 6.7 %collective-permute-done = bf16[1,32,384]{2,1,0:T(8,128)(2,1)S(1)} collective-permute-done((bf16[1,32,384]{2,1,0:T(8,128)(2,1)S(1)}, bf16[1,32,384]{2,1,0:T(8,128)(2,1)S(1)}, u32[]{:S(2)}, u32[]{:S(2)}) %collective-permute-start) | collective-permute-done | bytes 24608 | tf_op jit(solution)/shard_map/ppermute | solution.py:28
  208.0 4.3 collective-permute-start.2
  215.2 6.8 %copy.62 = bf16[64,12,9,384]{3,1,0,2:T(8,128)(2,1)} copy(bf16[64,12,9,384]{3,1,2,0:T(8,128)(2,1)} %all-to-all-done.1) | data formatting | bytes 10616832 | tf_op jit(solution)/shard_map/all_to_all | solution.py:197
  222.0 9.5 %reshape.494 = bf16[768,9,384]{2,0,1:T(8,128)(2,1)} reshape(bf16[64,12,9,384]{3,1,0,2:T(8,128)(2,1)} %copy.62) | data formatting | bytes 10616832 | tf_op jit(solution)/shard_map/reshape | solution.py:196
  231.5 1.7 fusion.78
  233.2 1.7 convolution_add_fusion.30
  239.9 2.5 collective-permute-start.3
  245.7 1.9 collective-permute-done.3
  249.1 10.5 %all-to-all-start.2 = ((f32[64,1,512]{2,1,0:T(1,128)}), f32[64,1,512]{2,1,0:T(1,128)S(1)}, u32[]{:S(2)}, u32[]{:S(2)}) async-start(f32[64,1,512]{2,1,0:T(1,128)} %broadcast_in_dim.15), calls=%async_computation.2 | async-start | bytes 262144 | tf_op jit(solution)/shard_map/all_to_all | solution.py:39
  261.1 1.6 collective-permute-start.9
  262.7 6.6 %all-to-all-done.2 = f32[64,1,512]{2,1,0:T(1,128)S(1)} async-done(((f32[64,1,512]{2,1,0:T(1,128)}), f32[64,1,512]{2,1,0:T(1,128)S(1)}, u32[]{:S(2)}, u32[]{:S(2)}) %all-to-all-start.2) | async-done | bytes 131104 | tf_op jit(solution)/shard_map/all_to_all | solution.py:39
  271.1 14.3 %all_to_all.30 = f32[64,1,512]{2,1,0:T(1,128)S(1)} all-to-all(f32[64,1,512]{2,1,0:T(1,128)S(1)} %broadcast_in_dim.16), channel_id=1, replica_groups=mesh['section'=4,'fsdp_0'=8,'fsdp_1'=2,'fsdp_2'=4] {'fsdp_0','fsdp_1','f..., dimensions={0} | all-to-all | bytes 262144 | tf_op jit(solution)/shard_map/all_to_all | solution.py:39
  286.4 1.9 collective-permute-start.5
  288.3 2.5 collective-permute-start.10
  290.8 4.5 collective-permute-done.4
  295.4 4.5 collective-permute-start.6
  309.0 1.9 copy.69
  310.9 1.9 dot_general.238
  312.8 1.9 copy.70
  314.7 1.9 dot_general.242
  316.6 1.9 copy.71
  318.5 1.9 dot_general.246
  320.4 1.9 copy.72
  322.3 1.9 dot_general.250
  324.2 1.9 copy.73
  326.1 1.9 dot_general.254
  328.9 1.9 dot_general.258
  332.2 1.5 bitcast_dynamic-update-slice_fusion.5
  336.9 11.2 %copy.75 = f32[8,4,2,12,9,384]{5,2,1,0,4,3:T(2,128)} copy(f32[8,4,2,12,9,384]{5,3,1,2,0,4:T(8,128)S(1)} %bitcast.231) | data formatting | bytes 21233664 | tf_op jit(solution)/shard_map/transpose | solution.py:58
  348.2 13.4 %reshape.546 = f32[64,12,9,384]{3,0,2,1:T(8,128)} reshape(f32[8,4,2,12,9,384]{5,2,1,0,4,3:T(2,128)} %copy.75) | data formatting | bytes 21233664 | tf_op jit(solution)/shard_map/reshape | solution.py:59
  365.4 5.9 %collective-permute-done.11 = bf16[1,32,384]{2,1,0:T(8,128)(2,1)S(1)} collective-permute-done((bf16[1,32,384]{2,1,0:T(8,128)(2,1)S(1)}, bf16[1,32,384]{2,1,0:T(8,128)(2,1)S(1)}, u32[]{:S(2)}, u32[]{:S(2)}) %collective-permute-start.11) | collective-permute-done | bytes 24608 | tf_op jit(solution)/shard_map/ppermute | solution.py:28
  371.6 1.6 fusion.79
  380.3 5.5 collective-permute-start.13
  389.2 84.6 %reduce-scatter.4.cloned.1.call-done = f32[8,12,9,384]{3,0,2,1:T(8,128)} async-done(((f32[64,12,9,384]{3,0,2,1:T(8,128)}), f32[8,12,9,384]{3,0,2,1:T(8,128)}) %reduce-scatter.4.cloned.1.call-update) | async-done | bytes 1327120 | tf_op jit(solution)/shard_map/reduce_scatter | solution.py:61
  476.4 8.4 %all-to-all-start.4 = ((f32[64,1,512]{2,1,0:T(1,128)}), f32[64,1,512]{2,1,0:T(1,128)S(1)}, u32[]{:S(2)}, u32[]{:S(2)}) async-start(f32[64,1,512]{2,1,0:T(1,128)} %broadcast_in_dim.17), calls=%async_computation.4 | async-start | bytes 262144 | tf_op jit(solution)/shard_map/all_to_all | solution.py:39
  486.4 8.2 %all-to-all-done.4 = f32[64,1,512]{2,1,0:T(1,128)S(1)} async-done(((f32[64,1,512]{2,1,0:T(1,128)}), f32[64,1,512]{2,1,0:T(1,128)S(1)}, u32[]{:S(2)}, u32[]{:S(2)}) %all-to-all-start.4) | async-done | bytes 131104 | tf_op jit(solution)/shard_map/all_to_all | solution.py:39
  495.0 32.6 %all-reduce.9.cloned.1.call-done = f32[8,12,9,384]{3,0,2,1:T(8,128)} async-done(((f32[8,12,9,384]{3,0,2,1:T(8,128)}), f32[8,12,9,384]{3,0,2,1:T(8,128)}) %all-reduce.9.cloned.1.call-update) | async-done | bytes 1327120
  527.6 2.2 constant_dynamic-slice_fusion.1
  530.2 2.3 fusion.7
  532.4 35.9 %all-reduce.11.cloned.1.call-done = f32[2,12,9,384]{3,0,2,1:T(2,128)} async-done(((f32[2,12,9,384]{3,0,2,1:T(2,128)}), f32[2,12,9,384]{3,0,2,1:T(2,128)}) %all-reduce.11.cloned.1.call-update) | async-done | bytes 331792
  568.3 1.7 constant_dynamic-slice_fusion
  (235 shorter events, 56.0 us)
Async XLA Ops:
  39.8 175.4 %all-to-all-start.1 = ((bf16[64,12,9,384]{3,1,2,0:T(8,128)(2,1)}), bf16[64,12,9,384]{3,1,2,0:T(8,128)(2,1)}, u32[]{:S(2)}, u32[]{:S(2)}) async-start(bf16[64,12,9,384]{3,1,2,0:T(8,128)(2,1)} %stack.4), calls=%async_computation.1 | async-start | bytes 14155776 | tf_op jit(solution)/shard_map/all_to_all | solution.py:197
  45.6 146.9 %collective-permute-start.8 = (bf16[1,32,384]{2,1,0:T(8,128)(2,1)S(1)}, bf16[1,32,384]{2,1,0:T(8,128)(2,1)S(1)}, u32[]{:S(2)}, u32[]{:S(2)}) collective-permute-start(bf16[1,32,384]{2,1,0:T(8,128)(2,1)S(1)} %get-tuple-element.87), channel_id=1, source_target_pairs={{1,0},{2,1},{3,2},{4,3},{5,4},{6,5},{7,6},{8,7},{9,8},{10,9},{11,1... | collective-permute-start | bytes 73736 | tf_op jit(solution)/shard_map/ppermute | solution.py:30
  51.1 144.1 %collective-permute-start.7 = (bf16[1,32,384]{2,1,0:T(8,128)(2,1)S(1)}, bf16[1,32,384]{2,1,0:T(8,128)(2,1)S(1)}, u32[]{:S(2)}, u32[]{:S(2)}) collective-permute-start(bf16[1,32,384]{2,1,0:T(8,128)(2,1)S(1)} %get-tuple-element.86), channel_id=1, source_target_pairs={{0,1},{1,2},{2,3},{3,4},{4,5},{5,6},{6,7},{7,8},{8,9},{9,10},{10,1... | collective-permute-start | bytes 73736 | tf_op jit(solution)/shard_map/ppermute | solution.py:28
  196.1 5.0 collective-permute-start.1
  201.0 6.9 %collective-permute-start = (bf16[1,32,384]{2,1,0:T(8,128)(2,1)S(1)}, bf16[1,32,384]{2,1,0:T(8,128)(2,1)S(1)}, u32[]{:S(2)}, u32[]{:S(2)}) collective-permute-start(bf16[1,32,384]{2,1,0:T(8,128)(2,1)S(1)} %get-tuple-element.90), channel_id=1, source_target_pairs={{0,1},{1,2},{2,3},{3,4},{4,5},{5,6},{6,7},{7,8},{8,9},{9,10},{10,1... | collective-permute-start | bytes 73736 | tf_op jit(solution)/shard_map/ppermute | solution.py:28
  208.0 5.5 collective-permute-start.2
  231.5 6.4 %copy-start = (bf16[768,9,384]{2,0,1:T(8,128)(2,1)S(1)}, bf16[768,9,384]{2,0,1:T(8,128)(2,1)}, u32[]{:S(2)}) copy-start(bf16[768,9,384]{2,0,1:T(8,128)(2,1)} %reshape.494) | copy-start | bytes 15925252
  235.0 4.5 copy-start.7
  236.5 6.0 %copy-start.12 = (bf16[8,32,384]{2,1,0:T(8,128)(2,1)S(1)}, bf16[8,32,384]{2,1,0:T(8,128)(2,1)}, u32[]{:S(2)}) copy-start(bf16[8,32,384]{2,1,0:T(8,128)(2,1)} %get-tuple-element.77) | copy-start | bytes 589828
  237.9 4.9 copy-start.14
  238.3 4.9 copy-start.11
  239.1 4.5 copy-start.10
  239.9 7.7 %collective-permute-start.3 = (bf16[256,384]{1,0:T(8,128)(2,1)S(1)}, bf16[256,384]{1,0:T(8,128)(2,1)S(1)}, u32[]{:S(2)}, u32[]{:S(2)}) collective-permute-start(bf16[256,384]{1,0:T(8,128)(2,1)S(1)} %fusion.5), channel_id=1, source_target_pairs={{0,128},{64,192},{128,0},{192,64},{1,129},{65,193},{129,1},{193,65... | collective-permute-start | bytes 589832 | tf_op jit(solution)/shard_map/ppermute | solution.py:18
  242.4 2.0 copy-start.9
  243.2 1.7 copy-start.8
  243.6 1.7 copy-start.13
  244.0 15.6 %copy-start.16 = (bf16[8,32,384]{2,1,0:T(8,128)(2,1)S(1)}, bf16[8,32,384]{2,1,0:T(8,128)(2,1)}, u32[]{:S(2)}) copy-start(bf16[8,32,384]{2,1,0:T(8,128)(2,1)} %get-tuple-element.72) | copy-start | bytes 589828
  244.9 41.3 %copy-start.15 = (bf16[256,384]{1,0:T(8,128)(2,1)S(1)}, bf16[256,384]{1,0:T(8,128)(2,1)}, u32[]{:S(2)}) copy-start(bf16[256,384]{1,0:T(8,128)(2,1)} %param.3) | copy-start | bytes 589828
  247.6 52.4 %copy-start.5 = (bf16[256,384]{1,0:T(8,128)(2,1)}, bf16[256,384]{1,0:T(8,128)(2,1)S(1)}, u32[]{:S(2)}) copy-start(bf16[256,384]{1,0:T(8,128)(2,1)S(1)} %collective-permute-done.3) | copy-start | bytes 589828
  249.1 20.2 %all-to-all-start.2 = ((f32[64,1,512]{2,1,0:T(1,128)}), f32[64,1,512]{2,1,0:T(1,128)S(1)}, u32[]{:S(2)}, u32[]{:S(2)}) async-start(f32[64,1,512]{2,1,0:T(1,128)} %broadcast_in_dim.15), calls=%async_computation.2 | async-start | bytes 262144 | tf_op jit(solution)/shard_map/all_to_all | solution.py:39
  259.6 214.2 %reduce-scatter.4.cloned.1.call-start = ((), (), s32[]{:S(2)}) async-start(), calls=%async_computation.6 | async-start | bytes 11943936 | tf_op jit(solution)/shard_map/reduce_scatter | solution.py:61
  261.1 8.9 %collective-permute-start.9 = (bf16[256,384]{1,0:T(8,128)(2,1)S(1)}, bf16[256,384]{1,0:T(8,128)(2,1)S(1)}, u32[]{:S(2)}, u32[]{:S(2)}) collective-permute-start(bf16[256,384]{1,0:T(8,128)(2,1)S(1)} %get-tuple-element.65), channel_id=1, source_target_pairs={{0,64},{64,0},{128,192},{192,128},{1,65},{65,1},{129,193},{193,129... | collective-permute-start | bytes 589832 | tf_op jit(solution)/shard_map/ppermute | solution.py:18
  286.4 4.4 collective-permute-start.5
  288.3 7.0 %collective-permute-start.4 = (bf16[1,32,384]{2,1,0:T(8,128)(2,1)S(1)}, bf16[1,32,384]{2,1,0:T(8,128)(2,1)S(1)}, u32[]{:S(2)}, u32[]{:S(2)}) collective-permute-start(bf16[1,32,384]{2,1,0:T(8,128)(2,1)S(1)} %get-tuple-element.88), channel_id=1, source_target_pairs={{0,1},{1,2},{2,3},{3,4},{4,5},{5,6},{6,7},{7,8},{8,9},{9,10},{10,1... | collective-permute-start | bytes 73736 | tf_op jit(solution)/shard_map/ppermute | solution.py:28
  288.3 11.6 %collective-permute-start.10 = (bf16[256,384]{1,0:T(8,128)(2,1)S(1)}, bf16[256,384]{1,0:T(8,128)(2,1)S(1)}, u32[]{:S(2)}, u32[]{:S(2)}) collective-permute-start(bf16[256,384]{1,0:T(8,128)(2,1)S(1)} %get-tuple-element.78), channel_id=1, source_target_pairs={{0,128},{64,192},{128,0},{192,64},{1,129},{65,193},{129,1},{193,65... | collective-permute-start | bytes 589832 | tf_op jit(solution)/shard_map/ppermute | solution.py:18
  295.4 5.7 collective-permute-start.6
  299.9 0.7 copy-start.17
  330.8 4.3 copy-start.1
  331.3 4.3 copy-start.2
  331.7 4.3 copy-start.3
  332.1 4.3 copy-start.4
  361.6 0.7 copy-start.19
  361.6 1.3 copy-start.18
  361.6 16.0 %slice-start = ((s8[5308416]{0:T(1024)(128)(4,1)}), s8[1114112]{0:T(1024)(128)(4,1)S(1)}, s32[]{:S(2)}) async-start(s8[5308416]{0:T(1024)(128)(4,1)} %bitcast.229), calls=%async_computation.9 | async-start | bytes 2228224
  361.6 166.0 %all-reduce.9.cloned.1.call-start = ((), (), s32[]{:S(2)}) async-start(), calls=%async_computation.7 | async-start | bytes 2654208
  361.7 3.7 collective-permute-start.12
  364.1 7.2 %collective-permute-start.11 = (bf16[1,32,384]{2,1,0:T(8,128)(2,1)S(1)}, bf16[1,32,384]{2,1,0:T(8,128)(2,1)S(1)}, u32[]{:S(2)}, u32[]{:S(2)}) collective-permute-start(bf16[1,32,384]{2,1,0:T(8,128)(2,1)S(1)} %get-tuple-element.82), channel_id=1, source_target_pairs={{0,1},{1,2},{2,3},{3,4},{4,5},{5,6},{6,7},{7,8},{8,9},{9,10},{10,1... | collective-permute-start | bytes 73736 | tf_op jit(solution)/shard_map/ppermute | solution.py:28
  371.3 6.3 %slice-start.1 = ((s8[5308416]{0:T(1024)(128)(4,1)}), s8[4194304]{0:T(1024)(128)(4,1)S(1)}, s32[]{:S(2)}) async-start(s8[5308416]{0:T(1024)(128)(4,1)} %bitcast.229), calls=%async_computation.10 | async-start | bytes 8388608
  380.3 93.5 %collective-permute-start.13 = (bf16[256,384]{1,0:T(8,128)(2,1)}, bf16[256,384]{1,0:T(8,128)(2,1)}, u32[]{:S(2)}, u32[]{:S(2)}) collective-permute-start(bf16[256,384]{1,0:T(8,128)(2,1)} %get-tuple-element.63), channel_id=1, source_target_pairs={{0,64},{64,0},{128,192},{192,128},{1,65},{65,1},{129,193},{193,129... | collective-permute-start | bytes 589832 | tf_op jit(solution)/shard_map/ppermute | solution.py:18
  388.0 142.2 %copy-start.6 = (bf16[256,384]{1,0:T(8,128)(2,1)S(1)}, bf16[256,384]{1,0:T(8,128)(2,1)}, u32[]{:S(2)}) copy-start(bf16[256,384]{1,0:T(8,128)(2,1)} %copy-done.5) | copy-start | bytes 589828
  476.4 18.2 %all-to-all-start.4 = ((f32[64,1,512]{2,1,0:T(1,128)}), f32[64,1,512]{2,1,0:T(1,128)S(1)}, u32[]{:S(2)}, u32[]{:S(2)}) async-start(f32[64,1,512]{2,1,0:T(1,128)} %broadcast_in_dim.17), calls=%async_computation.4 | async-start | bytes 262144 | tf_op jit(solution)/shard_map/all_to_all | solution.py:39
  484.8 83.5 %all-reduce.11.cloned.1.call-start = ((), (), s32[]{:S(2)}) async-start(), calls=%async_computation.8 | async-start | bytes 663552
Sparse Core Ops, SparseCore 0:
  361.8 111.9 reduce-scatter.3
  476.1 51.4 all-reduce.8
  530.2 38.0 all-reduce.10
